TPU v7x, 32 devices: a whole 2x2x4 slice. The times are simulated.
32 devices in a mesh: groups: 2 (over y), wide: 4 (over z), narrow: 4 (over x, core).
Axes of the slice: x: 2, y: 2, z: 4, core: 2. Of those that a mesh axis runs over, the one named last changes fastest.
Arguments:
- tokens: bfloat16 [512, 4096], P(('groups', 'wide'), 'narrow'), parts along dimension 0, may hold values from -6 to 6
- routes: int32 [512, 8], P(('groups', 'wide')), parts along dimension 0, may hold values from 0 to 15, all different within a row; in each aligned block of 64 rows (0 to 63, 64 to 127, ...) at most 40 rows name the same one
- gate_weights: float32 [512, 8], P(('groups', 'wide')), parts along dimension 0, may hold values from 0.05 to 1
- delta_of: int32 [16], replicated, may hold values from 0 to 15, each once
- base_gate: bfloat16 [4096, 1536], P('wide', 'narrow'), may hold values from -0.09375 to 0.09375
- base_up: bfloat16 [4096, 1536], P('wide', 'narrow'), may hold values from -0.09375 to 0.09375
- base_down: bfloat16 [1536, 4096], P('wide', 'narrow'), may hold values from -0.15625 to 0.15625
- gate_left: bfloat16 [16, 4096, 32], P('wide', 'narrow'), may hold values from -0.09375 to 0.09375
- gate_right: bfloat16 [16, 32, 1536], P('wide', None, 'narrow'), may hold values from -0.5 to 0.5
- up_left: bfloat16 [16, 4096, 32], P('wide', 'narrow'), may hold values from -0.09375 to 0.09375
- up_right: bfloat16 [16, 32, 1536], P('wide', None, 'narrow'), may hold values from -0.5 to 0.5
- down_left: bfloat16 [16, 1536, 32], P('wide', 'narrow'), may hold values from -0.15625 to 0.15625
- down_right: bfloat16 [16, 32, 4096], P('wide', None, 'narrow'), may hold values from -0.5 to 0.5
Outputs:
- mixed_out: bfloat16 [512, 4096], P(('groups', 'wide'), 'narrow'), parts along dimension 0
There are 2 independent parts, one for each index of `groups`. A program takes and returns all parts, laid end to end along the dimension named above; an argument that names none is the same for every part. Nothing has to cross between parts.
Inputs may be any that keep to these rules, and one draw needn't show every extreme that they name: `routes`: in each aligned block of 64 rows (the rows of one index of wide) no expert is named by more than 40 rows, and in some block some expert is named by exactly 40 rows.
All inputs are finite; a program needn't handle non-finite values.
Results may differ from a plain program's by a relative error of at most 0.0053.
Values may be sent and summed in bfloat16 or wider, within the bound.
A program may use at most 64 MiB of HBM per device.

v0:
```python
import jax
import jax.numpy as jnp
from jax import lax
from jax.sharding import PartitionSpec as P


def dot32(a, b):
    return jnp.dot(a, b, preferred_element_type=jnp.float32)


def shards(
    tokens,
    routes,
    gate_weights,
    delta_of,
    base_gate,
    base_up,
    base_down,
    gate_left,
    gate_right,
    up_left,
    up_right,
    down_left,
    down_right,
):
    exp_here, _, rank = gate_left.shape
    experts = delta_of.shape[0]
    mine = lax.axis_index("wide")
    bf16 = jnp.bfloat16
    expert_ids = lax.broadcasted_iota(jnp.int32, (1, 1, experts), 2)
    named = routes[:, :, None] == expert_ids
    delta_ids = jnp.sum(jnp.where(named, delta_of[None, None, :], 0), axis=2)
    weight_of = jnp.sum(
        jnp.where(delta_ids[:, :, None] == expert_ids, gate_weights[:, :, None], 0.0), axis=1
    )
    weights = lax.all_gather(weight_of, "wide", axis=0, tiled=True)
    weights = lax.dynamic_slice_in_dim(weights, mine * exp_here, exp_here, axis=1)
    rows = lax.all_gather(tokens, "wide", axis=0, tiled=True)
    full = lax.all_gather(rows, "narrow", axis=1, tiled=True)
    depth = base_gate.shape[0]
    part = lax.dynamic_slice_in_dim(full, mine * depth, depth, axis=1)
    base_both = jnp.concatenate([base_gate, base_up], axis=1)
    both = lax.psum(dot32(part, base_both), "wide")
    columns = base_gate.shape[1]
    lefts = jnp.concatenate([gate_left, up_left], axis=0)
    low = lax.psum(
        jnp.einsum("td,edr->ter", rows, lefts, preferred_element_type=jnp.float32), "narrow"
    )
    low = low.astype(bf16)
    mixed = 0.0
    thin = []
    for e in range(exp_here):
        gate = both[:, :columns] + dot32(low[:, e], gate_right[e])
        up = both[:, columns:] + dot32(low[:, exp_here + e], up_right[e])
        hidden = jax.nn.silu(gate) * up * weights[:, e : e + 1]
        mixed = mixed + hidden
        thin.append(dot32(hidden.astype(bf16), down_left[e]))
    mixed = lax.psum(mixed, "wide").astype(bf16)
    mixed_full = lax.all_gather(mixed, "narrow", axis=1, tiled=True)
    depth = base_down.shape[0]
    mixed_part = lax.dynamic_slice_in_dim(mixed_full, mine * depth, depth, axis=1)
    thin = lax.psum(jnp.concatenate(thin, axis=1), "narrow").astype(bf16)
    out = dot32(mixed_part, base_down) + dot32(thin, down_right.reshape(exp_here * rank, -1))
    out = lax.psum_scatter(out, "wide", scatter_dimension=0, tiled=True)
    return out.astype(bf16)


def solution(mesh):
    return jax.shard_map(
        shards,
        mesh=mesh,
        in_specs=(
            P(("groups", "wide"), "narrow"),
            P(("groups", "wide"), None),
            P(("groups", "wide"), None),
            P(),
            P("wide", "narrow"),
            P("wide", "narrow"),
            P("wide", "narrow"),
            P("wide", "narrow", None),
            P("wide", None, "narrow"),
            P("wide", "narrow", None),
            P("wide", None, "narrow"),
            P("wide", "narrow", None),
            P("wide", None, "narrow"),
        ),
        out_specs=P(("groups", "wide"), "narrow"),
        check_vma=False,
    )
```

profile of v0, /device:TPU:0, one launch (start us, length us, event | category | flops | bytes accessed | tf_op | source)
XLA Modules:
  0.0 180.8 jit_solution(11253720552039283029)
XLA Ops:
  6.5 0.0 copy-start
  6.5 0.0 all-gather.3.cloned.1.call-start
  6.5 19.5 %all_gather.12 = bf16[256,1024]{1,0:T(8,128)(2,1)} all-gather(bf16[64,1024]{1,0:T(8,128)(2,1)} %param.13), channel_id=1, replica_groups=mesh['groups'=2,'wide'=4,'narrow'=4] {'wide'}, dimensions={0}, use_global_device_ids=true | all-gather | bytes 655360 | tf_op jit(solution)/shard_map/all_gather | solution.py:38
  26.0 0.0 all-gather.3.cloned.1.call-update
  26.0 0.0 all-reduce.5.cloned.1.call-start
  26.1 0.0 copy-start.2
  26.1 0.0 copy-start.10
  26.1 0.0 copy-start.11
  26.1 22.3 %all-gather.3.cloned.1.call-done = bf16[256,4096]{1,0:T(8,128)(2,1)} async-done(((bf16[256,1024]{1,0:T(8,128)(2,1)}), bf16[256,4096]{1,0:T(8,128)(2,1)}) %all-gather.3.cloned.1.call-update) | async-done | bytes 2097168 | tf_op jit(solution)/shard_map/all_gather | solution.py:39
  48.5 3.0 %fusion = f32[256,768]{1,0:T(8,128)} fusion(bf16[1024,384]{1,0:T(8,128)(2,1)} %param.18, bf16[1024,384]{1,0:T(8,128)(2,1)} %param.17, bf16[256,4096]{1,0:T(8,128)(2,1)} %all-gather.3.cloned.1.call-done, s32[]{:T(128)S(6)} %select_n.17), kind=kOutput, calls=%fused_computation | convolution fusion | flops 405798912 | bytes 2883588 | tf_op jit(solution)/shard_map/dot_general | solution.py:8
  51.5 0.0 copy-start.7
  51.5 0.0 copy-start.9
  51.5 0.0 copy-start.8
  51.5 0.0 copy-start.4
  51.5 0.0 copy-start.6
  51.5 0.0 all-reduce.5.cloned.1.call-update
  51.5 0.0 reduce-scatter.2.cloned.1.call-start
  51.6 0.0 copy-done.2
  51.6 0.0 copy-done.10
  51.6 0.0 copy-done.11
  51.6 0.3 convolution_bitcast_fusion
  52.0 0.2 copy-done.7
  52.2 0.0 copy-done.9
  52.2 0.0 copy-start.5
  52.2 0.1 select_reduce_fusion.1
  52.3 0.0 copy-done.8
  52.3 13.5 %all-gather = f32[4,64,16]{1,2,0:T(8,128)S(1)} all-gather(f32[1,64,16]{1,2,0:T(8,128)S(1)} %bitcast.82), channel_id=1, replica_groups=mesh['groups'=2,'wide'=4,'narrow'=4] {'wide'}, dimensions={0}, use_global_device_ids=true | all-gather | bytes 20480 | tf_op jit(solution)/shard_map/all_gather | solution.py:36
  65.8 0.1 reshape.9
  65.9 13.8 %all-reduce.6 = bf16[256,8,32]{0,2,1:T(8,128)(2,1)S(1)} all-reduce(f32[256,8,32]{0,2,1:T(8,128)S(1)} %convolution_bitcast_fusion), channel_id=1, replica_groups=mesh['groups'=2,'wide'=4,'narrow'=4] {'narrow'}, use_global_device_ids=true, to_apply=%region_1.2 | all-reduce | flops 65536 | bytes 393216 | tf_op jit(solution)/shard_map/psum | solution.py:46
  79.8 15.9 %all-reduce.5.cloned.1.call-done = f32[256,768]{1,0:T(8,128)} async-done(((f32[256,768]{1,0:T(8,128)}), f32[256,768]{1,0:T(8,128)}) %all-reduce.5.cloned.1.call-update) | async-done | bytes 786448 | tf_op jit(solution)/shard_map/psum | solution.py:43
  95.7 0.0 copy-done.4
  95.7 0.0 copy-start.1
  95.7 1.3 convolution_add_fusion.4
  97.0 0.0 copy-done.6
  97.0 1.3 fusion.10
  98.2 0.0 copy-done.5
  98.3 0.2 fusion.19
  98.4 0.0 copy-done.1
  98.4 0.2 convolution_add_fusion.6
  98.7 0.3 fusion.9
  99.0 0.2 fusion.21
  99.1 0.3 convolution_add_fusion.8
  99.4 0.3 fusion.8
  99.7 0.2 fusion.23
  99.9 0.3 convolution_add_fusion.2
  100.1 0.0 copy-start.3
  100.1 0.3 add_add_fusion
  100.5 0.2 fusion.17
  100.7 11.8 %all-reduce.7 = bf16[256,128]{0,1:T(8,128)(2,1)S(1)} all-reduce(f32[256,128]{0,1:T(8,128)S(1)} %pad_maximum_fusion), channel_id=1, replica_groups=mesh['groups'=2,'wide'=4,'narrow'=4] {'narrow'}, use_global_device_ids=true, to_apply=%region_5.6 | all-reduce | flops 32768 | bytes 196608 | tf_op jit(solution)/shard_map/psum | solution.py:62
  112.5 25.1 %all-reduce.8 = bf16[256,384]{1,0:T(8,128)(2,1)S(1)} all-reduce(f32[256,384]{1,0:T(8,128)S(1)} %get-tuple-element.9), channel_id=1, replica_groups=mesh['groups'=2,'wide'=4,'narrow'=4] {'wide'}, use_global_device_ids=true, to_apply=%region_4.5 | all-reduce | flops 98304 | bytes 589824 | tf_op jit(solution)/shard_map/psum | solution.py:58
  137.6 7.4 %all_gather.15 = bf16[256,1536]{1,0:T(8,128)(2,1)S(1)} all-gather(bf16[256,384]{1,0:T(8,128)(2,1)S(1)} %all-reduce.8), channel_id=1, replica_groups=mesh['groups'=2,'wide'=4,'narrow'=4] {'narrow'}, dimensions={1}, use_global_device_ids=true | all-gather | bytes 983040 | tf_op jit(solution)/shard_map/all_gather | solution.py:59
  145.0 0.0 copy-done.3
  145.0 0.3 fusion.56
  145.3 0.0 copy-done
  145.3 1.4 convolution_add_fusion
  146.7 0.0 reduce-scatter.2.cloned.1.call-update
  146.8 25.9 %reduce-scatter.2.cloned.1.call-done = f32[64,1024]{1,0:T(8,128)} async-done(((f32[256,1024]{1,0:T(8,128)}), f32[64,1024]{1,0:T(8,128)}) %reduce-scatter.2.cloned.1.call-update) | async-done | bytes 262160 | tf_op jit(solution)/shard_map/reduce_scatter | solution.py:64
  172.7 1.6 convert_element_type.31
  (4 shorter events, 0.1 us)
Async XLA Ops:
  6.5 138.8 %copy-start = (bf16[384,1024]{1,0:T(8,128)(2,1)S(1)}, bf16[384,1024]{1,0:T(8,128)(2,1)}, u32[]{:S(2)}) copy-start(bf16[384,1024]{1,0:T(8,128)(2,1)} %param.19) | copy-start | bytes 2359300
  6.5 41.9 %all-gather.3.cloned.1.call-start = ((), (), s32[]{:S(2)}) async-start(), calls=%async_computation.1 | async-start | bytes 2621440 | tf_op jit(solution)/shard_map/all_gather | solution.py:39
  26.0 69.6 %all-reduce.5.cloned.1.call-start = ((), (), s32[]{:S(2)}) async-start(), calls=%async_computation.2 | async-start | bytes 1572864 | tf_op jit(solution)/shard_map/psum | solution.py:43
  26.1 25.5 %copy-start.2 = (bf16[256,1024]{1,0:T(8,128)(2,1)S(1)}, bf16[256,1024]{1,0:T(8,128)(2,1)}, u32[]{:S(2)}) copy-start(bf16[256,1024]{1,0:T(8,128)(2,1)} %all_gather.12) | copy-start | bytes 1572868
  26.1 25.5 %copy-start.10 = (bf16[4,1024,32]{1,2,0:T(8,128)(2,1)S(1)}, bf16[4,1024,32]{1,2,0:T(8,128)(2,1)}, u32[]{:S(2)}) copy-start(bf16[4,1024,32]{1,2,0:T(8,128)(2,1)} %param.22) | copy-start | bytes 786436
  26.1 25.5 %copy-start.11 = (bf16[4,1024,32]{1,2,0:T(8,128)(2,1)S(1)}, bf16[4,1024,32]{1,2,0:T(8,128)(2,1)}, u32[]{:S(2)}) copy-start(bf16[4,1024,32]{1,2,0:T(8,128)(2,1)} %param.20) | copy-start | bytes 786436
  51.5 0.7 copy-start.7
  51.5 0.7 copy-start.9
  51.5 0.8 copy-start.8
  51.5 44.2 %copy-start.4 = (bf16[4,32,384]{2,1,0:T(8,128)(2,1)S(1)}, bf16[4,32,384]{2,1,0:T(8,128)(2,1)}, u32[]{:S(2)}) copy-start(bf16[4,32,384]{2,1,0:T(8,128)(2,1)} %param.21) | copy-start | bytes 294916
  51.5 45.5 %copy-start.6 = (bf16[4,32,384]{2,1,0:T(8,128)(2,1)S(1)}, bf16[4,32,384]{2,1,0:T(8,128)(2,1)}, u32[]{:S(2)}) copy-start(bf16[4,32,384]{2,1,0:T(8,128)(2,1)} %param.23) | copy-start | bytes 294916
  51.5 121.1 %reduce-scatter.2.cloned.1.call-start = ((), (), s32[]{:S(2)}) async-start(), calls=%async_computation.3 | async-start | bytes 1310720 | tf_op jit(solution)/shard_map/reduce_scatter | solution.py:64
  52.2 46.1 %copy-start.5 = (bf16[4,384,32]{1,2,0:T(8,128)(2,1)S(1)}, bf16[4,384,32]{1,2,0:T(8,128)(2,1)}, u32[]{:S(2)}) copy-start(bf16[4,384,32]{1,2,0:T(8,128)(2,1)} %param.24) | copy-start | bytes 294916
  95.7 2.8 %copy-start.1 = (f32[256,768]{1,0:T(8,128)S(1)}, f32[256,768]{1,0:T(8,128)}, u32[]{:S(2)}) copy-start(f32[256,768]{1,0:T(8,128)} %all-reduce.5.cloned.1.call-done) | copy-start | bytes 2359300
  100.1 44.9 %copy-start.3 = (bf16[4,32,1024]{2,1,0:T(8,128)(2,1)S(1)}, bf16[4,32,1024]{2,1,0:T(8,128)(2,1)}, u32[]{:S(2)}) copy-start(bf16[4,32,1024]{2,1,0:T(8,128)(2,1)} %param.25) | copy-start | bytes 786436
Sparse Core Ops, SparseCore 0:
  26.2 22.2 all-gather.2
  51.6 43.9 all-reduce.4
  146.9 25.7 reduce-scatter.1
where the time goes:
time: 181 us
  blocking collectives  91.1 us (50%)
  waiting for transfers between devices  64.2 us (35%)
  between operations  13.4 us (7%)
  matrix products  9.89 us (5%)
    reduce_scatter x1, waiting for transfers between devices, shards(): out = lax.psum_scatter(out, 'wide', scatter_dimension=0, tiled=True)  25.9 us
    psum x1, blocking collectives, shards(): mixed = lax.psum(mixed, 'wide').astype(bf16)  25.1 us
    all_gather x1, waiting for transfers between devices, shards(): full = lax.all_gather(rows, 'narrow', axis=1, tiled=True)  22.3 us
    all_gather x1, blocking collectives, shards(): rows = lax.all_gather(tokens, 'wide', axis=0, tiled=True)  19.5 us
    psum x1, waiting for transfers between devices, shards(): both = lax.psum(dot32(part, base_both), 'wide')  15.9 us
    psum x1, blocking collectives, shards(): lax.psum(jnp.einsum('td,edr->ter', rows, lefts, preferred_element_type=jn...  13.8 us
    all_gather x1, blocking collectives, shards(): weights = lax.all_gather(weight_of, 'wide', axis=0, tiled=True)  13.5 us
    psum x1, blocking collectives, shards(): thin = lax.psum(jnp.concatenate(thin, axis=1), 'narrow').astype(bf16)  11.8 us
  transfers between devices with their start and end apart: 3, of which 3 were waited for; matrix products, arithmetic and copies ran while one was open for 0% of the time, Pallas kernels for 0%

commit v1 on v0

--- a/solution.py
+++ b/solution.py
@@ -40,7 +40,8 @@
     depth = base_gate.shape[0]
     part = lax.dynamic_slice_in_dim(full, mine * depth, depth, axis=1)
     base_both = jnp.concatenate([base_gate, base_up], axis=1)
-    both = lax.psum(dot32(part, base_both), "wide")
+    payload = dot32(part, base_both)
+    both = jnp.sum(lax.all_gather(payload, "wide"), axis=0)
     columns = base_gate.shape[1]
     lefts = jnp.concatenate([gate_left, up_left], axis=0)
     low = lax.psum(

time: 181 us -> 201 us (1.11)
  waiting for transfers between devices: 64.2 us -> 83.1 us
  other arithmetic: 1.75 us -> 3.95 us
  matrix products: 9.89 us -> 7.8 us
    all_gather x0 -> x1, waiting for transfers between devices: none -> 35 us  [shards(): both = jnp.sum(lax.all_gather(payload, 'wide'), axis=0)]
    psum x1 -> x0, waiting for transfers between devices: 15.9 us -> none  [shards(): both = lax.psum(dot32(part, base_both), 'wide')]
    reduce_sum x0 -> x1, other arithmetic: none -> 2.2 us  [shards(): both = jnp.sum(lax.all_gather(payload, 'wide'), axis=0)]
    dot_general x15, matrix products: 9.54 us -> 7.46 us  [dot32(): return jnp.dot(a, b, preferred_element_type=jnp.float32)]
where the time goes in v1:
time: 201 us
  blocking collectives  91.8 us (46%)
  waiting for transfers between devices  83.1 us (41%)
  between operations  13.4 us (7%)
  matrix products  7.8 us (4%)
  other arithmetic  3.95 us (2%)
    all_gather x1, waiting for transfers between devices, shards(): both = jnp.sum(lax.all_gather(payload, 'wide'), axis=0)  35 us
    reduce_scatter x1, waiting for transfers between devices, shards(): out = lax.psum_scatter(out, 'wide', scatter_dimension=0, tiled=True)  25.7 us
    psum x1, blocking collectives, shards(): mixed = lax.psum(mixed, 'wide').astype(bf16)  23.1 us
    all_gather x1, waiting for transfers between devices, shards(): full = lax.all_gather(rows, 'narrow', axis=1, tiled=True)  22.4 us
    all_gather x1, blocking collectives, shards(): rows = lax.all_gather(tokens, 'wide', axis=0, tiled=True)  19.5 us
    psum x1, blocking collectives, shards(): lax.psum(jnp.einsum('td,edr->ter', rows, lefts, preferred_element_type=jn...  14.6 us
    all_gather x1, blocking collectives, shards(): weights = lax.all_gather(weight_of, 'wide', axis=0, tiled=True)  13.2 us
    psum x1, blocking collectives, shards(): thin = lax.psum(jnp.concatenate(thin, axis=1), 'narrow').astype(bf16)  12.7 us
  transfers between devices with their start and end apart: 3, of which 3 were waited for; matrix products, arithmetic and copies ran while one was open for 0% of the time, Pallas kernels for 0%

profile of v1, /device:TPU:0, one launch (start us, length us, event | category | flops | bytes accessed | tf_op | source)
XLA Modules:
  0.0 200.8 jit_solution(4705600167929006232)
XLA Ops:
  6.5 0.0 copy-start
  6.5 0.0 all-gather.5.cloned.1.call-start
  6.5 19.5 %all_gather.18 = bf16[256,1024]{1,0:T(8,128)(2,1)} all-gather(bf16[64,1024]{1,0:T(8,128)(2,1)} %param.13), channel_id=1, replica_groups=mesh['groups'=2,'wide'=4,'narrow'=4] {'wide'}, dimensions={0}, use_global_device_ids=true | all-gather | bytes 655360 | tf_op jit(solution)/shard_map/all_gather | solution.py:38
  26.0 0.0 all-gather.5.cloned.1.call-update
  26.0 0.0 all-gather.7.cloned.1.call-start
  26.1 0.0 copy-start.1
  26.1 0.0 copy-start.9
  26.1 0.0 copy-start.10
  26.1 22.4 %all-gather.5.cloned.1.call-done = bf16[256,4096]{1,0:T(8,128)(2,1)} async-done(((bf16[256,1024]{1,0:T(8,128)(2,1)}), bf16[256,4096]{1,0:T(8,128)(2,1)}) %all-gather.5.cloned.1.call-update) | async-done | bytes 2097168 | tf_op jit(solution)/shard_map/all_gather | solution.py:39
  48.5 3.0 %fusion = f32[256,768]{1,0:T(8,128)} fusion(bf16[1024,384]{1,0:T(8,128)(2,1)} %param.18, bf16[1024,384]{1,0:T(8,128)(2,1)} %param.17, bf16[256,4096]{1,0:T(8,128)(2,1)} %all-gather.5.cloned.1.call-done, s32[]{:T(128)S(6)} %select_n.17), kind=kOutput, calls=%fused_computation | convolution fusion | flops 405798912 | bytes 2883588 | tf_op jit(solution)/shard_map/dot_general | solution.py:8
  51.4 0.0 copy-start.6
  51.5 0.0 copy-start.8
  51.5 0.0 copy-start.7
  51.5 0.0 all-gather.7.cloned.1.call-update
  51.5 0.0 reduce-scatter.2.cloned.1.call-start
  51.5 0.0 copy-done.1
  51.5 0.0 copy-done.9
  51.5 0.0 copy-done.10
  51.6 0.3 convolution_bitcast_fusion
  51.9 0.2 copy-done.6
  52.1 0.0 copy-done.8
  52.1 0.1 select_reduce_fusion.1
  52.2 0.0 copy-done.7
  52.3 13.2 %all-gather.1 = f32[4,64,16]{1,2,0:T(8,128)S(1)} all-gather(f32[1,64,16]{1,2,0:T(8,128)S(1)} %bitcast.84), channel_id=1, replica_groups=mesh['groups'=2,'wide'=4,'narrow'=4] {'wide'}, dimensions={0}, use_global_device_ids=true | all-gather | bytes 20480 | tf_op jit(solution)/shard_map/all_gather | solution.py:36
  65.5 0.1 reshape.10
  65.6 0.0 copy-start.3
  65.6 14.6 %all-reduce.3 = bf16[256,8,32]{0,2,1:T(8,128)(2,1)S(1)} all-reduce(f32[256,8,32]{0,2,1:T(8,128)S(1)} %convolution_bitcast_fusion), channel_id=1, replica_groups=mesh['groups'=2,'wide'=4,'narrow'=4] {'narrow'}, use_global_device_ids=true, to_apply=%region_1.2 | all-reduce | flops 65536 | bytes 393216 | tf_op jit(solution)/shard_map/psum | solution.py:47
  80.2 35.0 %all-gather.7.cloned.1.call-done = f32[1024,768]{1,0:T(8,128)} async-done(((f32[256,768]{1,0:T(8,128)}), f32[1024,768]{1,0:T(8,128)}) %all-gather.7.cloned.1.call-update) | async-done | bytes 3145744 | tf_op jit(solution)/shard_map/all_gather | solution.py:44
  115.2 2.2 %reduce_sum.27 = f32[256,768]{1,0:T(8,128)S(1)} reduce(f32[4,256,768]{2,1,0:T(8,128)} %bitcast.82, f32[]{:T(128)} %constant.21.clone.1), dimensions={0}, to_apply=%region_0.1 | reduce | flops 589824 | bytes 3932164 | tf_op jit(solution)/shard_map/reduce_sum | solution.py:44
  117.4 0.0 copy-done.3
  117.4 0.0 copy-start.5
  117.4 0.2 convolution_add_fusion.4
  117.6 0.2 convolution_add_fusion.8
  117.9 0.2 convolution_add_fusion.6
  118.1 0.2 convolution_add_fusion.2
  118.4 0.0 copy-done.5
  118.4 0.0 copy-start.4
  118.4 0.3 fusion.10
  118.7 0.3 fusion.9
  118.9 0.3 copy-done.4
  119.3 0.2 fusion.19
  119.4 0.2 fusion.21
  119.6 0.3 fusion.8
  119.9 0.2 fusion.23
  120.1 0.0 copy-start.2
  120.1 0.3 add_add_fusion
  120.4 0.2 fusion.17
  120.6 12.7 %all-reduce.4 = bf16[256,128]{0,1:T(8,128)(2,1)S(1)} all-reduce(f32[256,128]{0,1:T(8,128)S(1)} %pad_maximum_fusion), channel_id=1, replica_groups=mesh['groups'=2,'wide'=4,'narrow'=4] {'narrow'}, use_global_device_ids=true, to_apply=%region_5.6 | all-reduce | flops 32768 | bytes 196608 | tf_op jit(solution)/shard_map/psum | solution.py:63
  133.3 23.1 %all-reduce.5 = bf16[256,384]{1,0:T(8,128)(2,1)S(1)} all-reduce(f32[256,384]{1,0:T(8,128)S(1)} %get-tuple-element.9), channel_id=1, replica_groups=mesh['groups'=2,'wide'=4,'narrow'=4] {'wide'}, use_global_device_ids=true, to_apply=%region_4.5 | all-reduce | flops 98304 | bytes 589824 | tf_op jit(solution)/shard_map/psum | solution.py:59
  156.4 8.8 %all_gather.23 = bf16[256,1536]{1,0:T(8,128)(2,1)S(1)} all-gather(bf16[256,384]{1,0:T(8,128)(2,1)S(1)} %all-reduce.5), channel_id=1, replica_groups=mesh['groups'=2,'wide'=4,'narrow'=4] {'narrow'}, dimensions={1}, use_global_device_ids=true | all-gather | bytes 983040 | tf_op jit(solution)/shard_map/all_gather | solution.py:60
  165.2 0.0 copy-done.2
  165.2 0.3 fusion.56
  165.5 0.0 copy-done
  165.6 1.4 convolution_add_fusion
  167.0 0.0 reduce-scatter.2.cloned.1.call-update
  167.0 25.7 %reduce-scatter.2.cloned.1.call-done = f32[64,1024]{1,0:T(8,128)} async-done(((f32[256,1024]{1,0:T(8,128)}), f32[64,1024]{1,0:T(8,128)}) %reduce-scatter.2.cloned.1.call-update) | async-done | bytes 262160 | tf_op jit(solution)/shard_map/reduce_scatter | solution.py:65
  192.7 1.6 convert_element_type.31
  (4 shorter events, 0.1 us)
Async XLA Ops:
  6.5 159.0 %copy-start = (bf16[384,1024]{1,0:T(8,128)(2,1)S(1)}, bf16[384,1024]{1,0:T(8,128)(2,1)}, u32[]{:S(2)}) copy-start(bf16[384,1024]{1,0:T(8,128)(2,1)} %param.19) | copy-start | bytes 2359300
  6.5 41.9 %all-gather.5.cloned.1.call-start = ((), (), s32[]{:S(2)}) async-start(), calls=%async_computation.1 | async-start | bytes 2621440 | tf_op jit(solution)/shard_map/all_gather | solution.py:39
  26.0 89.1 %all-gather.7.cloned.1.call-start = ((), (), s32[]{:S(2)}) async-start(), calls=%async_computation.3 | async-start | bytes 3932160 | tf_op jit(solution)/shard_map/all_gather | solution.py:44
  26.1 25.4 %copy-start.1 = (bf16[256,1024]{1,0:T(8,128)(2,1)S(1)}, bf16[256,1024]{1,0:T(8,128)(2,1)}, u32[]{:S(2)}) copy-start(bf16[256,1024]{1,0:T(8,128)(2,1)} %all_gather.18) | copy-start | bytes 1572868
  26.1 25.4 %copy-start.9 = (bf16[4,1024,32]{1,2,0:T(8,128)(2,1)S(1)}, bf16[4,1024,32]{1,2,0:T(8,128)(2,1)}, u32[]{:S(2)}) copy-start(bf16[4,1024,32]{1,2,0:T(8,128)(2,1)} %param.22) | copy-start | bytes 786436
  26.1 25.4 %copy-start.10 = (bf16[4,1024,32]{1,2,0:T(8,128)(2,1)S(1)}, bf16[4,1024,32]{1,2,0:T(8,128)(2,1)}, u32[]{:S(2)}) copy-start(bf16[4,1024,32]{1,2,0:T(8,128)(2,1)} %param.20) | copy-start | bytes 786436
  51.4 0.7 copy-start.6
  51.5 0.7 copy-start.8
  51.5 0.8 copy-start.7
  51.5 141.2 %reduce-scatter.2.cloned.1.call-start = ((), (), s32[]{:S(2)}) async-start(), calls=%async_computation.2 | async-start | bytes 1310720 | tf_op jit(solution)/shard_map/reduce_scatter | solution.py:65
  65.6 51.7 %copy-start.3 = (bf16[4,32,384]{2,1,0:T(8,128)(2,1)S(1)}, bf16[4,32,384]{2,1,0:T(8,128)(2,1)}, u32[]{:S(2)}) copy-start(bf16[4,32,384]{2,1,0:T(8,128)(2,1)} %param.21) | copy-start | bytes 294916
  117.4 1.0 copy-start.5
  118.4 0.9 copy-start.4
  120.1 45.1 %copy-start.2 = (bf16[4,32,1024]{2,1,0:T(8,128)(2,1)S(1)}, bf16[4,32,1024]{2,1,0:T(8,128)(2,1)}, u32[]{:S(2)}) copy-start(bf16[4,32,1024]{2,1,0:T(8,128)(2,1)} %param.25) | copy-start | bytes 786436
Sparse Core Ops, SparseCore 0:
  26.1 22.2 all-gather.4
  51.6 63.5 all-gather.6
  167.1 25.5 reduce-scatter.1
